TPU v7x, 32 devices: a whole 2x2x4 slice. The times are simulated.
32 devices in a mesh: sim: 2 (over y), grp: 4 (over z), gz: 4 (over x, core).
Axes of the slice: x: 2, y: 2, z: 4, core: 2. Of those that a mesh axis runs over, the one named last changes fastest.
Arguments:
- fields: float32 [8, 2, 1024, 1024], P(None, None, 'sim', ('grp', 'gz')), may hold values from -6 to 6
- diffusivity: float32 [8], replicated, may hold values from 0.03 to 0.12
- velocity: float32 [2, 8], replicated, may hold values from -0.4 to 0.4
- coupling: float32 [8, 8], replicated, may hold values from -0.6 to 0.6
- basis_x: bfloat16 [1024, 128], replicated, may hold values from -0.1875 to 0.1875
- basis_y: bfloat16 [1024, 128], replicated, may hold values from -0.1875 to 0.1875
Outputs:
- fields_out: float32 [8, 2, 1024, 1024], P(None, None, 'sim', ('grp', 'gz'))
- gram_x: float32 [1024, 1024], P('sim', ('grp', 'gz'))
- gram_y: float32 [1024, 1024], P(('grp', 'gz'), 'sim')
- core: float32 [8, 2, 128, 128], P(None, None, 'sim', ('grp', 'gz'))
All inputs are finite; a program needn't handle non-finite values.
Results may differ from a plain program's by a relative error of at most 0.0003.
Values sent between devices are 32-bit elements; how exact they have to be, the bound alone decides.
No kernel may reach another device: no remote copies, remote signals or barrier semaphores. Data moves between devices by JAX's collectives and lax.ppermute only.
A program may use at most 64 MiB of HBM per device.

v0:
```python
import jax
import jax.numpy as jnp
from jax import lax
from jax.sharding import PartitionSpec as P

NY = 1024
RANK = 128
STEPS = 2
time_step = 1.0
highest = lax.Precision.HIGHEST


def with_halo(cells, sides, width):
    for axis, dim in sides:
        count = lax.axis_size(axis)
        head = lax.slice_in_dim(cells, 0, width, axis=dim)
        tail = lax.slice_in_dim(cells, cells.shape[dim] - width, cells.shape[dim], axis=dim)
        cells = jnp.concatenate(
            [
                lax.ppermute(tail, axis, [(i, (i + 1) % count) for i in range(count)]),
                cells,
                lax.ppermute(head, axis, [((i + 1) % count, i) for i in range(count)]),
            ],
            axis=dim,
        )
    return cells


def rates(state, diffusivity, velocity, coupling):
    padded = with_halo(state, (("sim", 2), (("grp", "gz"), 3)), 1)
    center = padded[:, :, 1:-1, 1:-1]
    x_plus = padded[:, :, 2:, 1:-1]
    x_minus = padded[:, :, :-2, 1:-1]
    y_plus = padded[:, :, 1:-1, 2:]
    y_minus = padded[:, :, 1:-1, :-2]
    z_plus = jnp.roll(center, -1, 1)
    z_minus = jnp.roll(center, 1, 1)
    lapl = -6.0 * center + z_plus + z_minus + x_plus + x_minus + y_plus + y_minus
    grad_x = (x_plus - x_minus) * 0.5
    grad_y = (y_plus - y_minus) * 0.5
    react = jnp.einsum("fg,gzxy->fzxy", coupling, jnp.tanh(center), precision=highest)
    return (
        diffusivity[:, None, None, None] * lapl
        - velocity[0][:, None, None, None] * grad_x
        - velocity[1][:, None, None, None] * grad_y
        + react
    )


def shards(fields, diffusivity, velocity, coupling, basis_x, basis_y):
    state = fields
    for repeat in range(STEPS):
        first = rates(state, diffusivity, velocity, coupling)
        second = rates(state + 0.5 * time_step * first, diffusivity, velocity, coupling)
        third = rates(state + 0.5 * time_step * second, diffusivity, velocity, coupling)
        fourth = rates(state + time_step * third, diffusivity, velocity, coupling)
        state = state + time_step / 6.0 * (first + 2.0 * second + 2.0 * third + fourth)
    nfield = state.shape[0]
    depth = state.shape[1]
    x_rows = state.shape[2]
    basis_xf = basis_x.astype(jnp.float32)
    basis_yf = basis_y.astype(jnp.float32)
    block = jnp.einsum(
        "fzxy,fzwy->xw", state, lax.all_gather(state, "sim", axis=2, tiled=True), precision=highest
    )
    gram_rows = block
    own_basis = lax.dynamic_slice_in_dim(basis_xf, lax.axis_index("sim") * x_rows, x_rows, 0)
    partial_proj = jnp.einsum("xr,fzxy->fzry", own_basis, state, precision=highest)
    projected = lax.psum_scatter(partial_proj, "sim", scatter_dimension=2, tiled=True)
    gram_x = lax.psum_scatter(gram_rows, ("grp", "gz"), scatter_dimension=1, tiled=True) / (
        nfield * depth * NY
    )
    rank_grp = RANK // lax.axis_size(("grp", "gz"))
    rank_cols_y = lax.dynamic_slice_in_dim(
        basis_yf, lax.axis_index(("grp", "gz")) * rank_grp, rank_grp, 1
    )
    incoming = lax.all_gather(projected, ("grp", "gz"), axis=3, tiled=True)
    block = jnp.einsum("fzry,fzrv->yv", projected, incoming, precision=highest)
    core_part = jnp.einsum("vs,fzrv->fzrs", rank_cols_y, incoming, precision=highest)
    gram_y = lax.psum_scatter(block, "sim", scatter_dimension=1, tiled=True) / (
        nfield * depth * RANK
    )
    return (state, gram_x, gram_y, core_part)


def solution(mesh):
    in_specs = (P(None, None, "sim", ("grp", "gz")), P(), P(), P(), P(), P())
    out_specs = (
        P(None, None, "sim", ("grp", "gz")),
        P("sim", ("grp", "gz")),
        P(("grp", "gz"), "sim"),
        P(None, None, "sim", ("grp", "gz")),
    )
    return jax.shard_map(shards, mesh=mesh, in_specs=in_specs, out_specs=out_specs, check_vma=False)
```

profile of v0, /device:TPU:0, one launch (start us, length us, event | category | flops | bytes accessed | tf_op | source)
XLA Modules:
  0.0 532.1 jit_solution(15932883289345783442)
XLA Ops:
  7.2 2.8 copy.61
  10.3 3.1 collective-permute-start
  13.6 12.5 %collective-permute-done = f32[8,2,1,64]{2,0,3,1:T(8,128)S(1)} collective-permute-done((f32[8,2,1,64]{2,0,3,1:T(8,128)S(1)}, f32[8,2,1,64]{2,0,3,1:T(8,128)S(1)}, u32[]{:S(2)}, u32[]{:S(2)}) %collective-permute-start) | collective-permute-done | bytes 4128 | tf_op jit(solution)/shard_map/ppermute | solution.py:22
  26.1 10.4 %collective-permute-done.1 = f32[8,2,1,64]{2,0,3,1:T(8,128)S(1)} collective-permute-done((f32[8,2,1,64]{2,0,3,1:T(8,128)S(1)}, f32[8,2,1,64]{2,0,3,1:T(8,128)S(1)}, u32[]{:S(2)}, u32[]{:S(2)}) %collective-permute-start.1) | collective-permute-done | bytes 4128 | tf_op jit(solution)/shard_map/ppermute | solution.py:20
  36.6 3.4 collective-permute-start.2
  41.6 4.4 collective-permute-done.3
  46.1 5.2 multiply_add_fusion.3
  51.5 1.6 collective-permute-start.4
  53.6 12.5 %collective-permute-done.4 = f32[8,2,1,64]{2,0,3,1:T(8,128)S(1)} collective-permute-done((f32[8,2,1,64]{2,0,3,1:T(8,128)S(1)}, f32[8,2,1,64]{2,0,3,1:T(8,128)S(1)}, u32[]{:S(2)}, u32[]{:S(2)}) %collective-permute-start.4) | collective-permute-done | bytes 4128 | tf_op jit(solution)/shard_map/ppermute | solution.py:22
  66.1 5.6 %collective-permute-done.5 = f32[8,2,1,64]{2,0,3,1:T(8,128)S(1)} collective-permute-done((f32[8,2,1,64]{2,0,3,1:T(8,128)S(1)}, f32[8,2,1,64]{2,0,3,1:T(8,128)S(1)}, u32[]{:S(2)}, u32[]{:S(2)}) %collective-permute-start.5) | collective-permute-done | bytes 4128 | tf_op jit(solution)/shard_map/ppermute | solution.py:20
  71.9 4.1 collective-permute-start.6
  77.7 4.6 collective-permute-done.7
  82.3 4.5 multiply_add_fusion.2
  87.0 1.6 collective-permute-start.8
  89.1 12.5 %collective-permute-done.8 = f32[8,2,1,64]{2,0,3,1:T(8,128)S(1)} collective-permute-done((f32[8,2,1,64]{2,0,3,1:T(8,128)S(1)}, f32[8,2,1,64]{2,0,3,1:T(8,128)S(1)}, u32[]{:S(2)}, u32[]{:S(2)}) %collective-permute-start.8) | collective-permute-done | bytes 4128 | tf_op jit(solution)/shard_map/ppermute | solution.py:22
  101.6 5.6 %collective-permute-done.9 = f32[8,2,1,64]{2,0,3,1:T(8,128)S(1)} collective-permute-done((f32[8,2,1,64]{2,0,3,1:T(8,128)S(1)}, f32[8,2,1,64]{2,0,3,1:T(8,128)S(1)}, u32[]{:S(2)}, u32[]{:S(2)}) %collective-permute-start.9) | collective-permute-done | bytes 4128 | tf_op jit(solution)/shard_map/ppermute | solution.py:20
  107.3 2.7 collective-permute-start.10
  110.2 1.5 collective-permute-done.10
  111.7 4.4 collective-permute-done.11
  116.1 4.9 copy_add_fusion
  121.2 1.6 collective-permute-start.12
  123.3 12.5 %collective-permute-done.12 = f32[8,2,1,64]{2,0,3,1:T(8,128)S(1)} collective-permute-done((f32[8,2,1,64]{2,0,3,1:T(8,128)S(1)}, f32[8,2,1,64]{2,0,3,1:T(8,128)S(1)}, u32[]{:S(2)}, u32[]{:S(2)}) %collective-permute-start.12) | collective-permute-done | bytes 4128 | tf_op jit(solution)/shard_map/ppermute | solution.py:22
  135.8 5.6 %collective-permute-done.13 = f32[8,2,1,64]{2,0,3,1:T(8,128)S(1)} collective-permute-done((f32[8,2,1,64]{2,0,3,1:T(8,128)S(1)}, f32[8,2,1,64]{2,0,3,1:T(8,128)S(1)}, u32[]{:S(2)}, u32[]{:S(2)}) %collective-permute-start.13) | collective-permute-done | bytes 4128 | tf_op jit(solution)/shard_map/ppermute | solution.py:20
  144.5 4.6 collective-permute-done.15
  149.2 5.1 fusion.36
  154.5 1.6 collective-permute-start.16
  156.6 12.5 %collective-permute-done.16 = f32[8,2,1,64]{2,0,3,1:T(8,128)S(1)} collective-permute-done((f32[8,2,1,64]{2,0,3,1:T(8,128)S(1)}, f32[8,2,1,64]{2,0,3,1:T(8,128)S(1)}, u32[]{:S(2)}, u32[]{:S(2)}) %collective-permute-start.16) | collective-permute-done | bytes 4128 | tf_op jit(solution)/shard_map/ppermute | solution.py:22
  169.1 5.6 %collective-permute-done.17 = f32[8,2,1,64]{2,0,3,1:T(8,128)S(1)} collective-permute-done((f32[8,2,1,64]{2,0,3,1:T(8,128)S(1)}, f32[8,2,1,64]{2,0,3,1:T(8,128)S(1)}, u32[]{:S(2)}, u32[]{:S(2)}) %collective-permute-start.17) | collective-permute-done | bytes 4128 | tf_op jit(solution)/shard_map/ppermute | solution.py:20
  176.0 1.5 collective-permute-done.18
  177.5 4.4 collective-permute-done.19
  181.9 5.4 %multiply_add_fusion.1 = (f32[8,2,512,64]{2,0,3,1:T(8,128)S(1)}, f32[8,2,512,64]{2,0,3,1:T(8,128)}) fusion(f32[8,2,512,64]{2,0,3,1:T(8,128)S(1)} %fusion.36, f32[8,8]{1,0:T(8,128)S(1)} %copy-done.9, f32[8]{0:T(128)S(1)} %get-tuple-element.65, f32[8]{0:T(128)S(1)} %get-tuple-element.64, f32[8,2,1,64]{2,0,3,1:T(8,128)S(1)} %collective-permute-done.16, ...), kind=kOutput, calls=%fused_computation.154 | convolution fusion | flops 63963136 | bytes 8462944 | tf_op jit(solution)/shard_map/fg,gzxy->fzxy/dot_general | solution.py:41
  187.5 1.6 collective-permute-start.20
  189.6 12.5 %collective-permute-done.20 = f32[8,2,1,64]{2,0,3,1:T(8,128)S(1)} collective-permute-done((f32[8,2,1,64]{2,0,3,1:T(8,128)S(1)}, f32[8,2,1,64]{2,0,3,1:T(8,128)S(1)}, u32[]{:S(2)}, u32[]{:S(2)}) %collective-permute-start.20) | collective-permute-done | bytes 4128 | tf_op jit(solution)/shard_map/ppermute | solution.py:22
  202.1 5.6 %collective-permute-done.21 = f32[8,2,1,64]{2,0,3,1:T(8,128)S(1)} collective-permute-done((f32[8,2,1,64]{2,0,3,1:T(8,128)S(1)}, f32[8,2,1,64]{2,0,3,1:T(8,128)S(1)}, u32[]{:S(2)}, u32[]{:S(2)}) %collective-permute-start.21) | collective-permute-done | bytes 4128 | tf_op jit(solution)/shard_map/ppermute | solution.py:20
  209.2 1.5 collective-permute-done.22
  210.7 4.4 collective-permute-done.23
  215.1 5.5 %multiply_add_fusion = (f32[8,2,512,64]{2,0,3,1:T(8,128)S(1)}, f32[8,2,512,64]{2,0,3,1:T(8,128)}) fusion(f32[8,2,512,64]{2,0,3,1:T(8,128)S(1)} %fusion.36, f32[8,8]{1,0:T(8,128)S(1)} %copy-done.9, f32[8,2,512,64]{2,0,3,1:T(8,128)S(1)} %get-tuple-element.72, f32[8]{0:T(128)S(1)} %get-tuple-element.65, f32[8]{0:T(128)S(1)} %get-tuple-element.64, ...), kind=kOutput, calls=%fused_computation.151 | convolution fusion | flops 63963136 | bytes 10560096 | tf_op jit(solution)/shard_map/fg,gzxy->fzxy/dot_general | solution.py:41
  220.9 1.6 collective-permute-start.24
  223.0 12.5 %collective-permute-done.24 = f32[8,2,1,64]{2,0,3,1:T(8,128)S(1)} collective-permute-done((f32[8,2,1,64]{2,0,3,1:T(8,128)S(1)}, f32[8,2,1,64]{2,0,3,1:T(8,128)S(1)}, u32[]{:S(2)}, u32[]{:S(2)}) %collective-permute-start.24) | collective-permute-done | bytes 4128 | tf_op jit(solution)/shard_map/ppermute | solution.py:22
  235.5 5.6 %collective-permute-done.25 = f32[8,2,1,64]{2,0,3,1:T(8,128)S(1)} collective-permute-done((f32[8,2,1,64]{2,0,3,1:T(8,128)S(1)}, f32[8,2,1,64]{2,0,3,1:T(8,128)S(1)}, u32[]{:S(2)}, u32[]{:S(2)}) %collective-permute-start.25) | collective-permute-done | bytes 4128 | tf_op jit(solution)/shard_map/ppermute | solution.py:20
  241.2 1.9 collective-permute-start.26
  244.8 4.8 collective-permute-done.27
  249.7 5.6 %fusion.158 = (f32[8,2,512,64]{2,0,3,1:T(8,128)S(1)}, f32[8,2,512,64]{2,0,3,1:T(8,128)}) fusion(f32[8,2,512,64]{2,0,3,1:T(8,128)S(1)} %fusion.36, f32[8,8]{1,0:T(8,128)S(1)} %copy-done.9, f32[8,2,512,64]{2,0,3,1:T(8,128)S(1)} %get-tuple-element.74, f32[8]{0:T(128)S(1)} %get-tuple-element.65, f32[8]{0:T(128)S(1)} %get-tuple-element.64, ...), kind=kOutput, calls=%fused_computation.229 | convolution fusion | flops 63438848 | bytes 10560096 | tf_op jit(solution)/shard_map/fg,gzxy->fzxy/dot_general | solution.py:41
  256.6 1.5 collective-permute-start.28
  258.7 12.7 %collective-permute-done.28 = f32[8,2,1,64]{2,0,3,1:T(8,128)S(1)} collective-permute-done((f32[8,2,1,64]{2,0,3,1:T(8,128)}, f32[8,2,1,64]{2,0,3,1:T(8,128)S(1)}, u32[]{:S(2)}, u32[]{:S(2)}) %collective-permute-start.28) | collective-permute-done | bytes 4128 | tf_op jit(solution)/shard_map/ppermute | solution.py:22
  271.4 5.6 %collective-permute-done.29 = f32[8,2,1,64]{2,0,3,1:T(8,128)S(1)} collective-permute-done((f32[8,2,1,64]{2,0,3,1:T(8,128)}, f32[8,2,1,64]{2,0,3,1:T(8,128)S(1)}, u32[]{:S(2)}, u32[]{:S(2)}) %collective-permute-start.29) | collective-permute-done | bytes 4128 | tf_op jit(solution)/shard_map/ppermute | solution.py:20
  277.1 1.8 collective-permute-start.30
  280.5 4.5 collective-permute-done.31
  285.0 8.8 %fusion.71 = f32[8,2,512,64]{2,0,3,1:T(8,128)S(1)} fusion(f32[8,2,512,64]{2,0,3,1:T(8,128)S(1)} %copy-done.4, f32[8,1,512,64]{2,0,3,1:T(8,128)S(1)} %get-tuple-element.35, f32[8,1,512,64]{2,0,3,1:T(8,128)S(1)} %get-tuple-element.34, f32[8,2,514,1]{2,0,3,1:T(8,128)S(1)} %collective-permute-done.30, f32[8,2,1,64]{2,0,3,1:T(8,128)S(1)} %collective-permute-done.28, ...), kind=kOutput, calls=%fused_computation.79 | convolution fusion | flops 66584576 | bytes 14754400 | tf_op jit(solution)/shard_map/fg,gzxy->fzxy/dot_general | solution.py:41
  293.9 1.9 convolution_bitcast_fusion
  295.8 1.9 copy.75
  297.7 1.8 reshape.20
  300.3 11.4 %reduce-scatter.10.cloned.1.call-done = f32[64,1024]{1,0:T(8,128)} async-done(((f32[128,1024]{1,0:T(8,128)}), f32[64,1024]{1,0:T(8,128)}) %reduce-scatter.10.cloned.1.call-update) | async-done | bytes 262160
  314.5 56.1 %all-gather.3.cloned.1.call-done = f32[8,2,1024,64]{2,0,3,1:T(8,128)} async-done(((f32[8,2,512,64]{2,0,3,1:T(8,128)}), f32[8,2,1024,64]{2,0,3,1:T(8,128)}) %all-gather.3.cloned.1.call-update) | async-done | bytes 4194320 | tf_op jit(solution)/shard_map/all_gather | solution.py:64
  370.5 9.7 %fusion.89 = f32[512,1024]{0,1:T(8,128)} fusion(f32[8,2,1024,64]{2,0,3,1:T(8,128)} %all-gather.3.cloned.1.call-done, f32[8,2,512,64]{2,0,3,1:T(8,128)S(1)} %copy-done.2), kind=kOutput, calls=%fused_computation.165 | convolution fusion | flops 6442450944 | bytes 8388608 | tf_op jit(solution)/shard_map/fzxy,fzwy->xw/dot_general | solution.py:63
  380.3 2.5 copy.69
  382.8 64.2 %all-gather.5.cloned.1.call-done = f32[8,2,64,1024]{2,0,1,3:T(8,128)} async-done(((f32[8,2,64,64]{2,0,1,3:T(8,128)}), f32[8,2,64,1024]{2,0,1,3:T(8,128)}) %all-gather.5.cloned.1.call-update) | async-done | bytes 4194320 | tf_op jit(solution)/shard_map/all_gather | solution.py:77
  447.0 6.9 %copy.66 = f32[8,2,64,1024]{3,2,1,0:T(8,128)} copy(f32[8,2,64,1024]{2,0,1,3:T(8,128)} %all-gather.5.cloned.1.call-done) | data formatting | bytes 8388608 | tf_op jit(solution)/shard_map/all_gather | solution.py:77
  453.9 5.8 %convolution_bitcast_fusion.1 = f32[64,1024]{1,0:T(8,128)} fusion(f32[8,2,64,1024]{3,2,1,0:T(8,128)} %copy.66, f32[8,2,64,64]{3,1,0,2:T(2,128)S(1)} %bitcast.93), kind=kOutput, calls=%fused_computation.167 | convolution fusion | flops 805306368 | bytes 4718592 | tf_op jit(solution)/shard_map/fzry,fzrv->yv/dot_general | solution.py:78
  459.7 51.4 %reduce-scatter.6.cloned.1.call-done = f32[512,64]{0,1:T(8,128)} async-done(((f32[512,1024]{0,1:T(8,128)}), f32[512,64]{0,1:T(8,128)}) %reduce-scatter.6.cloned.1.call-update) | async-done | bytes 131088 | tf_op jit(solution)/shard_map/reduce_scatter | solution.py:70
  511.0 1.6 broadcast_multiply_fusion.1
  512.6 5.5 %fusion.95 = f32[8,2,64,8]{2,3,1,0:T(8,128)} fusion(f32[8,2,64,1024]{3,2,1,0:T(8,128)} %copy.66, bf16[1024,128]{1,0:T(8,128)(2,1)S(1)} %copy-done.7, s32[]{:T(128)S(6)} %select_n.7), kind=kOutput, calls=%fused_computation.169 | convolution fusion | flops 100663296 | bytes 4489220 | tf_op jit(solution)/shard_map/vs,fzrv->fzrs/dot_general | solution.py:79
  518.0 5.8 %reduce-scatter.8.cloned.1.call-done = f32[64,512]{1,0:T(8,128)} async-done(((f32[64,1024]{1,0:T(8,128)}), f32[64,512]{1,0:T(8,128)}) %reduce-scatter.8.cloned.1.call-update) | async-done | bytes 131088 | tf_op jit(solution)/shard_map/reduce_scatter | solution.py:80
  523.8 1.6 broadcast_multiply_fusion
  (88 shorter events, 23.2 us)
Async XLA Ops:
  7.2 286.7 %copy-start = (bf16[1024,128]{1,0:T(8,128)(2,1)S(1)}, bf16[1024,128]{1,0:T(8,128)(2,1)}, u32[]{:S(2)}) copy-start(bf16[1024,128]{1,0:T(8,128)(2,1)} %param.10) | copy-start | bytes 786436
  7.2 304.5 %reduce-scatter.10.cloned.1.call-start = ((), (), s32[]{:S(2)}) async-start(), calls=%async_computation.7 | async-start | bytes 786432
  10.3 15.8 %collective-permute-start = (f32[8,2,1,64]{2,0,3,1:T(8,128)S(1)}, f32[8,2,1,64]{2,0,3,1:T(8,128)S(1)}, u32[]{:S(2)}, u32[]{:S(2)}) collective-permute-start(f32[8,2,1,64]{2,0,3,1:T(8,128)S(1)} %get-tuple-element.61), channel_id=1, source_target_pairs={{16,0},{0,16},{17,1},{1,17},{18,2},{2,18},{19,3},{3,19},{20,4},{4,... | collective-permute-start | bytes 12296 | tf_op jit(solution)/shard_map/ppermute | solution.py:22
  13.3 23.2 %collective-permute-start.1 = (f32[8,2,1,64]{2,0,3,1:T(8,128)S(1)}, f32[8,2,1,64]{2,0,3,1:T(8,128)S(1)}, u32[]{:S(2)}, u32[]{:S(2)}) collective-permute-start(f32[8,2,1,64]{2,0,3,1:T(8,128)S(1)} %get-tuple-element.60), channel_id=1, source_target_pairs={{0,16},{16,0},{1,17},{17,1},{2,18},{18,2},{3,19},{19,3},{4,20},{20... | collective-permute-start | bytes 12296 | tf_op jit(solution)/shard_map/ppermute | solution.py:20
  13.6 26.4 %copy-start.8 = (f32[2,8]{1,0:T(2,128)S(1)}, f32[2,8]{1,0:T(2,128)}, u32[]{:S(2)}) copy-start(f32[2,8]{1,0:T(2,128)} %param.8) | copy-start | bytes 196
  13.6 26.4 %copy-start.6 = (f32[8,2,512,64]{2,3,1,0:T(8,128)S(1)}, f32[8,2,512,64]{2,3,1,0:T(8,128)}, u32[]{:S(2)}) copy-start(f32[8,2,512,64]{2,3,1,0:T(8,128)} %param.6) | copy-start | bytes 6291460
  36.6 5.1 collective-permute-start.2
  40.0 6.1 %collective-permute-start.3 = (f32[8,2,514,1]{2,0,3,1:T(8,128)S(1)}, f32[8,2,514,1]{2,0,3,1:T(8,128)S(1)}, u32[]{:S(2)}, u32[]{:S(2)}) collective-permute-start(f32[8,2,514,1]{2,0,3,1:T(8,128)S(1)} %get-tuple-element.30), channel_id=1, source_target_pairs={{0,1},{1,2},{2,3},{3,4},{4,5},{5,6},{6,7},{7,8},{8,9},{9,10},{10,1... | collective-permute-start | bytes 98696 | tf_op jit(solution)/shard_map/ppermute | solution.py:20
  40.0 6.1 %copy-start.9 = (f32[8,8]{1,0:T(8,128)S(1)}, f32[8,8]{1,0:T(8,128)}, u32[]{:S(2)}) copy-start(f32[8,8]{1,0:T(8,128)} %param.9) | copy-start | bytes 772
  40.0 6.1 %copy-start.10 = (f32[8]{0:T(128)S(1)}, f32[8]{0:T(128)}, u32[]{:S(2)}) copy-start(f32[8]{0:T(128)} %param.7) | copy-start | bytes 100
  51.5 14.6 %collective-permute-start.4 = (f32[8,2,1,64]{2,0,3,1:T(8,128)S(1)}, f32[8,2,1,64]{2,0,3,1:T(8,128)S(1)}, u32[]{:S(2)}, u32[]{:S(2)}) collective-permute-start(f32[8,2,1,64]{2,0,3,1:T(8,128)S(1)} %get-tuple-element.57), channel_id=1, source_target_pairs={{16,0},{0,16},{17,1},{1,17},{18,2},{2,18},{19,3},{3,19},{20,4},{4,... | collective-permute-start | bytes 12296 | tf_op jit(solution)/shard_map/ppermute | solution.py:22
  53.1 18.6 %collective-permute-start.5 = (f32[8,2,1,64]{2,0,3,1:T(8,128)S(1)}, f32[8,2,1,64]{2,0,3,1:T(8,128)S(1)}, u32[]{:S(2)}, u32[]{:S(2)}) collective-permute-start(f32[8,2,1,64]{2,0,3,1:T(8,128)S(1)} %get-tuple-element.56), channel_id=1, source_target_pairs={{0,16},{16,0},{1,17},{17,1},{2,18},{18,2},{3,19},{19,3},{4,20},{20... | collective-permute-start | bytes 12296 | tf_op jit(solution)/shard_map/ppermute | solution.py:20
  71.9 5.8 %collective-permute-start.6 = (f32[8,2,514,1]{2,0,3,1:T(8,128)S(1)}, f32[8,2,514,1]{2,0,3,1:T(8,128)S(1)}, u32[]{:S(2)}, u32[]{:S(2)}) collective-permute-start(f32[8,2,514,1]{2,0,3,1:T(8,128)S(1)} %get-tuple-element.29), channel_id=1, source_target_pairs={{1,0},{2,1},{3,2},{4,3},{5,4},{6,5},{7,6},{8,7},{9,8},{10,9},{11,1... | collective-permute-start | bytes 98696 | tf_op jit(solution)/shard_map/ppermute | solution.py:22
  76.0 6.3 %collective-permute-start.7 = (f32[8,2,514,1]{2,0,3,1:T(8,128)S(1)}, f32[8,2,514,1]{2,0,3,1:T(8,128)S(1)}, u32[]{:S(2)}, u32[]{:S(2)}) collective-permute-start(f32[8,2,514,1]{2,0,3,1:T(8,128)S(1)} %get-tuple-element.28), channel_id=1, source_target_pairs={{0,1},{1,2},{2,3},{3,4},{4,5},{5,6},{6,7},{7,8},{8,9},{9,10},{10,1... | collective-permute-start | bytes 98696 | tf_op jit(solution)/shard_map/ppermute | solution.py:20
  87.0 14.6 %collective-permute-start.8 = (f32[8,2,1,64]{2,0,3,1:T(8,128)S(1)}, f32[8,2,1,64]{2,0,3,1:T(8,128)S(1)}, u32[]{:S(2)}, u32[]{:S(2)}) collective-permute-start(f32[8,2,1,64]{2,0,3,1:T(8,128)S(1)} %get-tuple-element.53), channel_id=1, source_target_pairs={{16,0},{0,16},{17,1},{1,17},{18,2},{2,18},{19,3},{3,19},{20,4},{4,... | collective-permute-start | bytes 12296 | tf_op jit(solution)/shard_map/ppermute | solution.py:22
  88.6 18.6 %collective-permute-start.9 = (f32[8,2,1,64]{2,0,3,1:T(8,128)S(1)}, f32[8,2,1,64]{2,0,3,1:T(8,128)S(1)}, u32[]{:S(2)}, u32[]{:S(2)}) collective-permute-start(f32[8,2,1,64]{2,0,3,1:T(8,128)S(1)} %get-tuple-element.52), channel_id=1, source_target_pairs={{0,16},{16,0},{1,17},{17,1},{2,18},{18,2},{3,19},{19,3},{4,20},{20... | collective-permute-start | bytes 12296 | tf_op jit(solution)/shard_map/ppermute | solution.py:20
  107.3 4.3 collective-permute-start.10
  110.0 6.1 %collective-permute-start.11 = (f32[8,2,514,1]{2,0,3,1:T(8,128)S(1)}, f32[8,2,514,1]{2,0,3,1:T(8,128)S(1)}, u32[]{:S(2)}, u32[]{:S(2)}) collective-permute-start(f32[8,2,514,1]{2,0,3,1:T(8,128)S(1)} %get-tuple-element.26), channel_id=1, source_target_pairs={{0,1},{1,2},{2,3},{3,4},{4,5},{5,6},{6,7},{7,8},{8,9},{9,10},{10,1... | collective-permute-start | bytes 98696 | tf_op jit(solution)/shard_map/ppermute | solution.py:20
  121.2 14.6 %collective-permute-start.12 = (f32[8,2,1,64]{2,0,3,1:T(8,128)S(1)}, f32[8,2,1,64]{2,0,3,1:T(8,128)S(1)}, u32[]{:S(2)}, u32[]{:S(2)}) collective-permute-start(f32[8,2,1,64]{2,0,3,1:T(8,128)S(1)} %get-tuple-element.49), channel_id=1, source_target_pairs={{16,0},{0,16},{17,1},{1,17},{18,2},{2,18},{19,3},{3,19},{20,4},{4,... | collective-permute-start | bytes 12296 | tf_op jit(solution)/shard_map/ppermute | solution.py:22
  122.8 18.6 %collective-permute-start.13 = (f32[8,2,1,64]{2,0,3,1:T(8,128)S(1)}, f32[8,2,1,64]{2,0,3,1:T(8,128)S(1)}, u32[]{:S(2)}, u32[]{:S(2)}) collective-permute-start(f32[8,2,1,64]{2,0,3,1:T(8,128)S(1)} %get-tuple-element.48), channel_id=1, source_target_pairs={{0,16},{16,0},{1,17},{17,1},{2,18},{18,2},{3,19},{19,3},{4,20},{20... | collective-permute-start | bytes 12296 | tf_op jit(solution)/shard_map/ppermute | solution.py:20
  141.5 3.0 collective-permute-start.14
  142.9 6.3 %collective-permute-start.15 = (f32[8,2,514,1]{2,0,3,1:T(8,128)S(1)}, f32[8,2,514,1]{2,0,3,1:T(8,128)S(1)}, u32[]{:S(2)}, u32[]{:S(2)}) collective-permute-start(f32[8,2,514,1]{2,0,3,1:T(8,128)S(1)} %get-tuple-element.24), channel_id=1, source_target_pairs={{0,1},{1,2},{2,3},{3,4},{4,5},{5,6},{6,7},{7,8},{8,9},{9,10},{10,1... | collective-permute-start | bytes 98696 | tf_op jit(solution)/shard_map/ppermute | solution.py:20
  154.3 95.4 %copy-start.3 = (f32[8,2,512,64]{2,0,3,1:T(8,128)}, f32[8,2,512,64]{2,0,3,1:T(8,128)S(1)}, u32[]{:S(2)}) copy-start(f32[8,2,512,64]{2,0,3,1:T(8,128)S(1)} %fusion.36) | copy-start | bytes 6291460
  154.5 14.6 %collective-permute-start.16 = (f32[8,2,1,64]{2,0,3,1:T(8,128)S(1)}, f32[8,2,1,64]{2,0,3,1:T(8,128)S(1)}, u32[]{:S(2)}, u32[]{:S(2)}) collective-permute-start(f32[8,2,1,64]{2,0,3,1:T(8,128)S(1)} %get-tuple-element.45), channel_id=1, source_target_pairs={{16,0},{0,16},{17,1},{1,17},{18,2},{2,18},{19,3},{3,19},{20,4},{4,... | collective-permute-start | bytes 12296 | tf_op jit(solution)/shard_map/ppermute | solution.py:22
  156.1 18.6 %collective-permute-start.17 = (f32[8,2,1,64]{2,0,3,1:T(8,128)S(1)}, f32[8,2,1,64]{2,0,3,1:T(8,128)S(1)}, u32[]{:S(2)}, u32[]{:S(2)}) collective-permute-start(f32[8,2,1,64]{2,0,3,1:T(8,128)S(1)} %get-tuple-element.44), channel_id=1, source_target_pairs={{0,16},{16,0},{1,17},{17,1},{2,18},{18,2},{3,19},{19,3},{4,20},{20... | collective-permute-start | bytes 12296 | tf_op jit(solution)/shard_map/ppermute | solution.py:20
  174.8 2.6 collective-permute-start.18
  175.8 6.1 %collective-permute-start.19 = (f32[8,2,514,1]{2,0,3,1:T(8,128)S(1)}, f32[8,2,514,1]{2,0,3,1:T(8,128)S(1)}, u32[]{:S(2)}, u32[]{:S(2)}) collective-permute-start(f32[8,2,514,1]{2,0,3,1:T(8,128)S(1)} %get-tuple-element.22), channel_id=1, source_target_pairs={{0,1},{1,2},{2,3},{3,4},{4,5},{5,6},{6,7},{7,8},{8,9},{9,10},{10,1... | collective-permute-start | bytes 98696 | tf_op jit(solution)/shard_map/ppermute | solution.py:20
  187.5 14.6 %collective-permute-start.20 = (f32[8,2,1,64]{2,0,3,1:T(8,128)S(1)}, f32[8,2,1,64]{2,0,3,1:T(8,128)S(1)}, u32[]{:S(2)}, u32[]{:S(2)}) collective-permute-start(f32[8,2,1,64]{2,0,3,1:T(8,128)S(1)} %get-tuple-element.41), channel_id=1, source_target_pairs={{16,0},{0,16},{17,1},{1,17},{18,2},{2,18},{19,3},{3,19},{20,4},{4,... | collective-permute-start | bytes 12296 | tf_op jit(solution)/shard_map/ppermute | solution.py:22
  189.1 18.6 %collective-permute-start.21 = (f32[8,2,1,64]{2,0,3,1:T(8,128)S(1)}, f32[8,2,1,64]{2,0,3,1:T(8,128)S(1)}, u32[]{:S(2)}, u32[]{:S(2)}) collective-permute-start(f32[8,2,1,64]{2,0,3,1:T(8,128)S(1)} %get-tuple-element.40), channel_id=1, source_target_pairs={{0,16},{16,0},{1,17},{17,1},{2,18},{18,2},{3,19},{19,3},{4,20},{20... | collective-permute-start | bytes 12296 | tf_op jit(solution)/shard_map/ppermute | solution.py:20
  207.9 2.8 collective-permute-start.22
  209.0 6.1 %collective-permute-start.23 = (f32[8,2,514,1]{2,0,3,1:T(8,128)S(1)}, f32[8,2,514,1]{2,0,3,1:T(8,128)S(1)}, u32[]{:S(2)}, u32[]{:S(2)}) collective-permute-start(f32[8,2,514,1]{2,0,3,1:T(8,128)S(1)} %get-tuple-element.20), channel_id=1, source_target_pairs={{0,1},{1,2},{2,3},{3,4},{4,5},{5,6},{6,7},{7,8},{8,9},{9,10},{10,1... | collective-permute-start | bytes 98696 | tf_op jit(solution)/shard_map/ppermute | solution.py:20
  220.9 14.6 %collective-permute-start.24 = (f32[8,2,1,64]{2,0,3,1:T(8,128)S(1)}, f32[8,2,1,64]{2,0,3,1:T(8,128)S(1)}, u32[]{:S(2)}, u32[]{:S(2)}) collective-permute-start(f32[8,2,1,64]{2,0,3,1:T(8,128)S(1)} %get-tuple-element.37), channel_id=1, source_target_pairs={{16,0},{0,16},{17,1},{1,17},{18,2},{2,18},{19,3},{3,19},{20,4},{4,... | collective-permute-start | bytes 12296 | tf_op jit(solution)/shard_map/ppermute | solution.py:22
  222.5 18.6 %collective-permute-start.25 = (f32[8,2,1,64]{2,0,3,1:T(8,128)S(1)}, f32[8,2,1,64]{2,0,3,1:T(8,128)S(1)}, u32[]{:S(2)}, u32[]{:S(2)}) collective-permute-start(f32[8,2,1,64]{2,0,3,1:T(8,128)S(1)} %get-tuple-element.36), channel_id=1, source_target_pairs={{0,16},{16,0},{1,17},{17,1},{2,18},{18,2},{3,19},{19,3},{4,20},{20... | collective-permute-start | bytes 12296 | tf_op jit(solution)/shard_map/ppermute | solution.py:20
  241.2 3.6 collective-permute-start.26
  243.2 6.5 %collective-permute-start.27 = (f32[8,2,514,1]{2,0,3,1:T(8,128)S(1)}, f32[8,2,514,1]{2,0,3,1:T(8,128)S(1)}, u32[]{:S(2)}, u32[]{:S(2)}) collective-permute-start(f32[8,2,514,1]{2,0,3,1:T(8,128)S(1)} %get-tuple-element.18), channel_id=1, source_target_pairs={{0,1},{1,2},{2,3},{3,4},{4,5},{5,6},{6,7},{7,8},{8,9},{9,10},{10,1... | collective-permute-start | bytes 98696 | tf_op jit(solution)/shard_map/ppermute | solution.py:20
  255.3 23.6 %copy-start.5 = (f32[8,2,512,64]{2,0,3,1:T(8,128)}, f32[8,2,512,64]{2,0,3,1:T(8,128)S(1)}, u32[]{:S(2)}) copy-start(f32[8,2,512,64]{2,0,3,1:T(8,128)S(1)} %get-tuple-element.76) | copy-start | bytes 6291460
  256.6 14.8 %collective-permute-start.28 = (f32[8,2,1,64]{2,0,3,1:T(8,128)}, f32[8,2,1,64]{2,0,3,1:T(8,128)S(1)}, u32[]{:S(2)}, u32[]{:S(2)}) collective-permute-start(f32[8,2,1,64]{2,0,3,1:T(8,128)} %get-tuple-element.33), channel_id=1, source_target_pairs={{16,0},{0,16},{17,1},{1,17},{18,2},{2,18},{19,3},{3,19},{20,4},{4,... | collective-permute-start | bytes 12296 | tf_op jit(solution)/shard_map/ppermute | solution.py:22
  258.2 18.9 %collective-permute-start.29 = (f32[8,2,1,64]{2,0,3,1:T(8,128)}, f32[8,2,1,64]{2,0,3,1:T(8,128)S(1)}, u32[]{:S(2)}, u32[]{:S(2)}) collective-permute-start(f32[8,2,1,64]{2,0,3,1:T(8,128)} %get-tuple-element.32), channel_id=1, source_target_pairs={{0,16},{16,0},{1,17},{17,1},{2,18},{18,2},{3,19},{19,3},{4,20},{20... | collective-permute-start | bytes 12296 | tf_op jit(solution)/shard_map/ppermute | solution.py:20
  277.0 8.0 %copy-start.12 = (f32[8,2,512,64]{2,0,3,1:T(8,128)S(1)}, f32[8,2,512,64]{2,0,3,1:T(8,128)}, u32[]{:S(2)}) copy-start(f32[8,2,512,64]{2,0,3,1:T(8,128)} %get-tuple-element.75) | copy-start | bytes 6291460
  277.1 3.4 collective-permute-start.30
  278.9 6.1 %copy-start.4 = (f32[8,2,512,64]{2,0,3,1:T(8,128)S(1)}, f32[8,2,512,64]{2,0,3,1:T(8,128)}, u32[]{:S(2)}) copy-start(f32[8,2,512,64]{2,0,3,1:T(8,128)} %copy-done.3) | copy-start | bytes 6291460
  278.9 6.1 %copy-start.11 = (f32[8,2,512,64]{2,0,3,1:T(8,128)S(1)}, f32[8,2,512,64]{2,0,3,1:T(8,128)}, u32[]{:S(2)}) copy-start(f32[8,2,512,64]{2,0,3,1:T(8,128)} %get-tuple-element.73) | copy-start | bytes 6291460
  278.9 6.1 %collective-permute-start.31 = (f32[8,2,514,1]{2,0,3,1:T(8,128)S(1)}, f32[8,2,514,1]{2,0,3,1:T(8,128)S(1)}, u32[]{:S(2)}, u32[]{:S(2)}) collective-permute-start(f32[8,2,514,1]{2,0,3,1:T(8,128)S(1)} %get-tuple-element.16), channel_id=1, source_target_pairs={{0,1},{1,2},{2,3},{3,4},{4,5},{5,6},{6,7},{7,8},{8,9},{9,10},{10,1... | collective-permute-start | bytes 98696 | tf_op jit(solution)/shard_map/ppermute | solution.py:20
  293.8 3.8 copy-start.1
  299.5 71.0 %copy-start.2 = (f32[8,2,512,64]{2,0,3,1:T(8,128)S(1)}, f32[8,2,512,64]{2,0,3,1:T(8,128)}, u32[]{:S(2)}) copy-start(f32[8,2,512,64]{2,0,3,1:T(8,128)} %copy-done.1) | copy-start | bytes 6291460
  299.5 71.0 %all-gather.3.cloned.1.call-start = ((), (), s32[]{:S(2)}) async-start(), calls=%async_computation.3 | async-start | bytes 6291456 | tf_op jit(solution)/shard_map/all_gather | solution.py:64
  300.2 146.8 %all-gather.5.cloned.1.call-start = ((), (), s32[]{:S(2)}) async-start(), calls=%async_computation.5 | async-start | bytes 8912896 | tf_op jit(solution)/shard_map/all_gather | solution.py:77
  314.2 196.8 %reduce-scatter.6.cloned.1.call-start = ((), (), s32[]{:S(2)}) async-start(), calls=%async_computation.4 | async-start | bytes 2228224 | tf_op jit(solution)/shard_map/reduce_scatter | solution.py:70
  380.2 143.6 %reduce-scatter.8.cloned.1.call-start = ((), (), s32[]{:S(2)}) async-start(), calls=%async_computation.6 | async-start | bytes 393216 | tf_op jit(solution)/shard_map/reduce_scatter | solution.py:80
  453.9 58.7 %copy-start.7 = (bf16[1024,128]{1,0:T(8,128)(2,1)S(1)}, bf16[1024,128]{1,0:T(8,128)(2,1)}, u32[]{:S(2)}) copy-start(bf16[1024,128]{1,0:T(8,128)(2,1)} %param.11) | copy-start | bytes 786436
Sparse Core Ops, SparseCore 0:
  299.6 11.9 reduce-scatter.9
  313.8 56.7 all-gather.2
  372.7 74.2 all-gather.4
  450.6 60.3 reduce-scatter.5
  513.1 10.6 reduce-scatter.7
where the time goes:
time: 539 us; the launch traced here: 532 us
  waiting for transfers between devices  387 us (72%)
  matrix products  68 us (13%)
  starting transfers between devices  36.2 us (7%)
  local copies, waits for them, and re-layouts  23 us (4%)
  between operations  14.3 us (3%)
    ppermute x16, waiting for transfers between devices, with_halo(): lax.ppermute(head, axis, [((i + 1) % count, i) for i in range(count)])  111 us
    ppermute x16, waiting for transfers between devices, with_halo(): lax.ppermute(tail, axis, [(i, (i + 1) % count) for i in range(count)])  86 us
    all_gather x1, waiting for transfers between devices, shards(): incoming = lax.all_gather(projected, ('grp', 'gz'), axis=3, tiled=True)  64.2 us
    all_gather x1, waiting for transfers between devices, shards(): lax.all_gather(state, 'sim', axis=2, tiled=True)  56.1 us
    reduce_scatter x1, waiting for transfers between devices, shards(): lax.psum_scatter(gram_rows, ('grp', 'gz'), scatter_dimension=1, tiled=True)  51.4 us
    dot_general x8, matrix products, rates(): jnp.einsum('fg,gzxy->fzxy', coupling, jnp.tanh(center), precision=highest)  45.2 us
    ppermute x16, starting transfers between devices, with_halo(): lax.ppermute(head, axis, [((i + 1) % count, i) for i in range(count)])  31.4 us
    unnamed x6, waiting for transfers between devices  12.1 us
  transfers between devices with their start and end apart: 37, of which 37 were waited for; matrix products, arithmetic and copies ran while one was open for 7% of the time, Pallas kernels for 0%

commit v1 on v0

--- a/solution.py
+++ b/solution.py
@@ -2,6 +2,7 @@
 import jax.numpy as jnp
 from jax import lax
 from jax.sharding import PartitionSpec as P
+from jax.lax import axis_index, axis_size, ppermute
 
 NY = 1024
 RANK = 128
@@ -60,8 +61,20 @@
     x_rows = state.shape[2]
     basis_xf = basis_x.astype(jnp.float32)
     basis_yf = basis_y.astype(jnp.float32)
+
+    def note_strings_for(ax_name, payload):
+        small, arr_now, p_next = (axis_size(ax_name), axis_index(ax_name), payload.shape[2])
+        clean, t_next = (payload, 1)
+        while t_next < small:
+            by_rank = []
+            for rr in range(small):
+                by_rank.append((rr, (rr - t_next) % small))
+            clean = jnp.concatenate([clean, ppermute(clean, ax_name, by_rank)], axis=2)
+            t_next = 2 * t_next
+        return jnp.roll(clean, arr_now * p_next, 2)
+
     block = jnp.einsum(
-        "fzxy,fzwy->xw", state, lax.all_gather(state, "sim", axis=2, tiled=True), precision=highest
+        "fzxy,fzwy->xw", state, note_strings_for("sim", payload=state), precision=highest
     )
     gram_rows = block
     own_basis = lax.dynamic_slice_in_dim(basis_xf, lax.axis_index("sim") * x_rows, x_rows, 0)

time: 539 us -> 479 us (0.89)
  waiting for transfers between devices: 387 us -> 327 us
    all_gather x1 -> x0, waiting for transfers between devices: 56.1 us -> none  [shards(): lax.all_gather(state, 'sim', axis=2, tiled=True)]
    all_gather x1, waiting for transfers between devices: 64.2 us -> 13.5 us  [shards(): incoming = lax.all_gather(projected, ('grp', 'gz'), axis=3, tiled=True)]
    ppermute x0 -> x1, waiting for transfers between devices: none -> 46.9 us  [note_strings_for(): clean = jnp.concatenate([clean, ppermute(clean, ax_name, by_rank)], axis=2)]
    unnamed x31 -> x29, local copies, waits for them, and re-layouts: 10.4 us -> 12.1 us
    unnamed x6 -> x5, waiting for transfers between devices: 12.1 us -> 12.2 us
where the time goes in v1:
time: 479 us; the launch traced here: 472 us
  waiting for transfers between devices  327 us (68%)
  matrix products  65 us (14%)
  starting transfers between devices  36.8 us (8%)
  local copies, waits for them, and re-layouts  24.5 us (5%)
  between operations  14.3 us (3%)
    ppermute x16, waiting for transfers between devices, with_halo(): lax.ppermute(head, axis, [((i + 1) % count, i) for i in range(count)])  111 us
    ppermute x16, waiting for transfers between devices, with_halo(): lax.ppermute(tail, axis, [(i, (i + 1) % count) for i in range(count)])  86 us
    reduce_scatter x1, waiting for transfers between devices, shards(): lax.psum_scatter(gram_rows, ('grp', 'gz'), scatter_dimension=1, tiled=True)  51.5 us
    ppermute x1, waiting for transfers between devices, note_strings_for(): clean = jnp.concatenate([clean, ppermute(clean, ax_name, by_rank)], axis=2)  46.9 us
    dot_general x8, matrix products, rates(): jnp.einsum('fg,gzxy->fzxy', coupling, jnp.tanh(center), precision=highest)  42.2 us
    ppermute x16, starting transfers between devices, with_halo(): lax.ppermute(head, axis, [((i + 1) % count, i) for i in range(count)])  31.4 us
    all_gather x1, waiting for transfers between devices, shards(): incoming = lax.all_gather(projected, ('grp', 'gz'), axis=3, tiled=True)  13.5 us
    unnamed x5, waiting for transfers between devices  12.2 us
  transfers between devices with their start and end apart: 37, of which 37 were waited for; matrix products, arithmetic and copies ran while one was open for 7% of the time, Pallas kernels for 0%

profile of v1, /device:TPU:0, one launch (start us, length us, event | category | flops | bytes accessed | tf_op | source)
XLA Modules:
  0.0 472.4 jit_solution(10738134227841243436)
XLA Ops:
  7.2 2.8 copy.61
  10.3 3.1 collective-permute-start
  13.6 12.5 %collective-permute-done = f32[8,2,1,64]{2,0,3,1:T(8,128)S(1)} collective-permute-done((f32[8,2,1,64]{2,0,3,1:T(8,128)S(1)}, f32[8,2,1,64]{2,0,3,1:T(8,128)S(1)}, u32[]{:S(2)}, u32[]{:S(2)}) %collective-permute-start) | collective-permute-done | bytes 4128 | tf_op jit(solution)/shard_map/ppermute | solution.py:23
  26.1 10.4 %collective-permute-done.1 = f32[8,2,1,64]{2,0,3,1:T(8,128)S(1)} collective-permute-done((f32[8,2,1,64]{2,0,3,1:T(8,128)S(1)}, f32[8,2,1,64]{2,0,3,1:T(8,128)S(1)}, u32[]{:S(2)}, u32[]{:S(2)}) %collective-permute-start.1) | collective-permute-done | bytes 4128 | tf_op jit(solution)/shard_map/ppermute | solution.py:21
  36.6 3.4 collective-permute-start.2
  41.6 4.4 collective-permute-done.3
  46.1 5.3 %multiply_add_fusion.3 = (f32[8,2,512,64]{2,0,3,1:T(8,128)S(1)}, f32[8,2,512,64]{2,0,3,1:T(8,128)S(1)}) fusion(f32[8,2,512,64]{2,3,1,0:T(8,128)S(1)} %copy-done.3, f32[8,2,512,64]{2,3,1,0:T(8,128)S(1)} %tanh.24, f32[8,8]{1,0:T(8,128)S(1)} %copy-done.8, f32[8]{0:T(128)S(1)} %get-tuple-element.65, f32[8]{0:T(128)S(1)} %get-tuple-element.64, ...), kind=kOutput, calls=%fused_computation.171 | convolution fusion | flops 63963136 | bytes 12657248 | tf_op jit(solution)/shard_map/fg,gzxy->fzxy/dot_general | solution.py:42
  51.6 1.6 collective-permute-start.4
  53.7 12.5 %collective-permute-done.4 = f32[8,2,1,64]{2,0,3,1:T(8,128)S(1)} collective-permute-done((f32[8,2,1,64]{2,0,3,1:T(8,128)S(1)}, f32[8,2,1,64]{2,0,3,1:T(8,128)S(1)}, u32[]{:S(2)}, u32[]{:S(2)}) %collective-permute-start.4) | collective-permute-done | bytes 4128 | tf_op jit(solution)/shard_map/ppermute | solution.py:23
  66.2 5.6 %collective-permute-done.5 = f32[8,2,1,64]{2,0,3,1:T(8,128)S(1)} collective-permute-done((f32[8,2,1,64]{2,0,3,1:T(8,128)S(1)}, f32[8,2,1,64]{2,0,3,1:T(8,128)S(1)}, u32[]{:S(2)}, u32[]{:S(2)}) %collective-permute-start.5) | collective-permute-done | bytes 4128 | tf_op jit(solution)/shard_map/ppermute | solution.py:21
  71.9 4.1 collective-permute-start.6
  77.7 4.6 collective-permute-done.7
  82.3 4.5 multiply_add_fusion.2
  87.0 1.6 collective-permute-start.8
  89.1 12.5 %collective-permute-done.8 = f32[8,2,1,64]{2,0,3,1:T(8,128)S(1)} collective-permute-done((f32[8,2,1,64]{2,0,3,1:T(8,128)S(1)}, f32[8,2,1,64]{2,0,3,1:T(8,128)S(1)}, u32[]{:S(2)}, u32[]{:S(2)}) %collective-permute-start.8) | collective-permute-done | bytes 4128 | tf_op jit(solution)/shard_map/ppermute | solution.py:23
  101.6 5.6 %collective-permute-done.9 = f32[8,2,1,64]{2,0,3,1:T(8,128)S(1)} collective-permute-done((f32[8,2,1,64]{2,0,3,1:T(8,128)S(1)}, f32[8,2,1,64]{2,0,3,1:T(8,128)S(1)}, u32[]{:S(2)}, u32[]{:S(2)}) %collective-permute-start.9) | collective-permute-done | bytes 4128 | tf_op jit(solution)/shard_map/ppermute | solution.py:21
  107.4 2.7 collective-permute-start.10
  110.2 1.5 collective-permute-done.10
  111.7 4.4 collective-permute-done.11
  116.1 4.9 %copy_add_fusion = (f32[8,2,512,64]{2,0,3,1:T(8,128)S(1)}, f32[8,2,512,64]{2,0,3,1:T(8,128)S(1)}) fusion(f32[8,2,512,64]{2,3,1,0:T(8,128)S(1)} %copy-done.3, f32[8,8]{1,0:T(8,128)S(1)} %copy-done.8, f32[8,2,512,64]{2,0,3,1:T(8,128)S(1)} %get-tuple-element.68, f32[8]{0:T(128)S(1)} %get-tuple-element.65, f32[8]{0:T(128)S(1)} %get-tuple-element.64, ...), kind=kOutput, calls=%fused_computation.219 | convolution fusion | flops 63438848 | bytes 10560096 | tf_op jit(solution)/shard_map/fg,gzxy->fzxy/dot_general | solution.py:42
  121.2 1.6 collective-permute-start.12
  123.3 12.5 %collective-permute-done.12 = f32[8,2,1,64]{2,0,3,1:T(8,128)S(1)} collective-permute-done((f32[8,2,1,64]{2,0,3,1:T(8,128)S(1)}, f32[8,2,1,64]{2,0,3,1:T(8,128)S(1)}, u32[]{:S(2)}, u32[]{:S(2)}) %collective-permute-start.12) | collective-permute-done | bytes 4128 | tf_op jit(solution)/shard_map/ppermute | solution.py:23
  135.8 5.6 %collective-permute-done.13 = f32[8,2,1,64]{2,0,3,1:T(8,128)S(1)} collective-permute-done((f32[8,2,1,64]{2,0,3,1:T(8,128)S(1)}, f32[8,2,1,64]{2,0,3,1:T(8,128)S(1)}, u32[]{:S(2)}, u32[]{:S(2)}) %collective-permute-start.13) | collective-permute-done | bytes 4128 | tf_op jit(solution)/shard_map/ppermute | solution.py:21
  144.5 4.6 collective-permute-done.15
  149.2 5.1 %fusion.39 = f32[8,2,512,64]{2,0,3,1:T(8,128)S(1)} fusion(f32[8,1,512,64]{2,0,3,1:T(8,128)S(1)} %get-tuple-element.51, f32[8,1,512,64]{2,0,3,1:T(8,128)S(1)} %get-tuple-element.50, f32[8,2,514,1]{2,0,3,1:T(8,128)S(1)} %collective-permute-done.14, f32[8,2,1,64]{2,0,3,1:T(8,128)S(1)} %collective-permute-done.12, f32[8,2,512,64]{2,0,3,1:T(8,128)S(1)} %get-tuple-element.70, ...), kind=kOutput, calls=%fused_computation.51 | convolution fusion | flops 66584576 | bytes 14754400 | tf_op jit(solution)/shard_map/fg,gzxy->fzxy/dot_general | solution.py:42
  154.5 1.6 collective-permute-start.16
  156.6 12.5 %collective-permute-done.16 = f32[8,2,1,64]{2,0,3,1:T(8,128)S(1)} collective-permute-done((f32[8,2,1,64]{2,0,3,1:T(8,128)S(1)}, f32[8,2,1,64]{2,0,3,1:T(8,128)S(1)}, u32[]{:S(2)}, u32[]{:S(2)}) %collective-permute-start.16) | collective-permute-done | bytes 4128 | tf_op jit(solution)/shard_map/ppermute | solution.py:23
  169.1 5.6 %collective-permute-done.17 = f32[8,2,1,64]{2,0,3,1:T(8,128)S(1)} collective-permute-done((f32[8,2,1,64]{2,0,3,1:T(8,128)S(1)}, f32[8,2,1,64]{2,0,3,1:T(8,128)S(1)}, u32[]{:S(2)}, u32[]{:S(2)}) %collective-permute-start.17) | collective-permute-done | bytes 4128 | tf_op jit(solution)/shard_map/ppermute | solution.py:21
  176.0 1.5 collective-permute-done.18
  177.5 4.4 collective-permute-done.19
  181.9 5.3 %multiply_add_fusion.1 = (f32[8,2,512,64]{2,0,3,1:T(8,128)S(1)}, f32[8,2,512,64]{2,0,3,1:T(8,128)}) fusion(f32[8,2,512,64]{2,0,3,1:T(8,128)S(1)} %fusion.39, f32[8,8]{1,0:T(8,128)S(1)} %copy-done.8, f32[8]{0:T(128)S(1)} %get-tuple-element.65, f32[8]{0:T(128)S(1)} %get-tuple-element.64, f32[8,2,1,64]{2,0,3,1:T(8,128)S(1)} %collective-permute-done.16, ...), kind=kOutput, calls=%fused_computation.161 | convolution fusion | flops 63963136 | bytes 8462944 | tf_op jit(solution)/shard_map/fg,gzxy->fzxy/dot_general | solution.py:42
  187.5 1.6 collective-permute-start.20
  189.6 12.5 %collective-permute-done.20 = f32[8,2,1,64]{2,0,3,1:T(8,128)S(1)} collective-permute-done((f32[8,2,1,64]{2,0,3,1:T(8,128)S(1)}, f32[8,2,1,64]{2,0,3,1:T(8,128)S(1)}, u32[]{:S(2)}, u32[]{:S(2)}) %collective-permute-start.20) | collective-permute-done | bytes 4128 | tf_op jit(solution)/shard_map/ppermute | solution.py:23
  202.1 5.6 %collective-permute-done.21 = f32[8,2,1,64]{2,0,3,1:T(8,128)S(1)} collective-permute-done((f32[8,2,1,64]{2,0,3,1:T(8,128)S(1)}, f32[8,2,1,64]{2,0,3,1:T(8,128)S(1)}, u32[]{:S(2)}, u32[]{:S(2)}) %collective-permute-start.21) | collective-permute-done | bytes 4128 | tf_op jit(solution)/shard_map/ppermute | solution.py:21
  209.1 1.5 collective-permute-done.22
  210.6 4.4 collective-permute-done.23
  215.1 5.6 %multiply_add_fusion = (f32[8,2,512,64]{2,0,3,1:T(8,128)S(1)}, f32[8,2,512,64]{2,0,3,1:T(8,128)}) fusion(f32[8,2,512,64]{2,0,3,1:T(8,128)S(1)} %fusion.39, f32[8,8]{1,0:T(8,128)S(1)} %copy-done.8, f32[8,2,512,64]{2,0,3,1:T(8,128)S(1)} %get-tuple-element.72, f32[8]{0:T(128)S(1)} %get-tuple-element.65, f32[8]{0:T(128)S(1)} %get-tuple-element.64, ...), kind=kOutput, calls=%fused_computation.158 | convolution fusion | flops 63963136 | bytes 10560096 | tf_op jit(solution)/shard_map/fg,gzxy->fzxy/dot_general | solution.py:42
  220.9 1.6 collective-permute-start.24
  223.0 12.5 %collective-permute-done.24 = f32[8,2,1,64]{2,0,3,1:T(8,128)S(1)} collective-permute-done((f32[8,2,1,64]{2,0,3,1:T(8,128)S(1)}, f32[8,2,1,64]{2,0,3,1:T(8,128)S(1)}, u32[]{:S(2)}, u32[]{:S(2)}) %collective-permute-start.24) | collective-permute-done | bytes 4128 | tf_op jit(solution)/shard_map/ppermute | solution.py:23
  235.5 5.6 %collective-permute-done.25 = f32[8,2,1,64]{2,0,3,1:T(8,128)S(1)} collective-permute-done((f32[8,2,1,64]{2,0,3,1:T(8,128)S(1)}, f32[8,2,1,64]{2,0,3,1:T(8,128)S(1)}, u32[]{:S(2)}, u32[]{:S(2)}) %collective-permute-start.25) | collective-permute-done | bytes 4128 | tf_op jit(solution)/shard_map/ppermute | solution.py:21
  241.2 1.9 collective-permute-start.26
  244.8 4.8 %collective-permute-done.27 = f32[8,2,514,1]{2,0,3,1:T(8,128)S(1)} collective-permute-done((f32[8,2,514,1]{2,0,3,1:T(8,128)S(1)}, f32[8,2,514,1]{2,0,3,1:T(8,128)S(1)}, u32[]{:S(2)}, u32[]{:S(2)}) %collective-permute-start.27) | collective-permute-done | bytes 32928 | tf_op jit(solution)/shard_map/ppermute | solution.py:21
  249.7 5.6 %fusion.161 = (f32[8,2,512,64]{2,0,3,1:T(8,128)S(1)}, f32[8,2,512,64]{2,0,3,1:T(8,128)}) fusion(f32[8,2,512,64]{2,0,3,1:T(8,128)S(1)} %fusion.39, f32[8,8]{1,0:T(8,128)S(1)} %copy-done.8, f32[8,2,512,64]{2,0,3,1:T(8,128)S(1)} %get-tuple-element.74, f32[8]{0:T(128)S(1)} %get-tuple-element.65, f32[8]{0:T(128)S(1)} %get-tuple-element.64, ...), kind=kOutput, calls=%fused_computation.236 | convolution fusion | flops 63438848 | bytes 10560096 | tf_op jit(solution)/shard_map/fg,gzxy->fzxy/dot_general | solution.py:42
  255.2 1.4 copy-done.1
  257.8 1.5 collective-permute-start.28
  259.8 12.7 %collective-permute-done.28 = f32[8,2,1,64]{2,0,3,1:T(8,128)S(1)} collective-permute-done((f32[8,2,1,64]{2,0,3,1:T(8,128)}, f32[8,2,1,64]{2,0,3,1:T(8,128)S(1)}, u32[]{:S(2)}, u32[]{:S(2)}) %collective-permute-start.28) | collective-permute-done | bytes 4128 | tf_op jit(solution)/shard_map/ppermute | solution.py:23
  272.5 5.6 %collective-permute-done.29 = f32[8,2,1,64]{2,0,3,1:T(8,128)S(1)} collective-permute-done((f32[8,2,1,64]{2,0,3,1:T(8,128)}, f32[8,2,1,64]{2,0,3,1:T(8,128)S(1)}, u32[]{:S(2)}, u32[]{:S(2)}) %collective-permute-start.29) | collective-permute-done | bytes 4128 | tf_op jit(solution)/shard_map/ppermute | solution.py:21
  279.0 1.8 collective-permute-start.30
  281.0 1.5 collective-permute-done.30
  282.4 4.5 collective-permute-done.31
  286.9 5.9 %fusion.74 = f32[8,2,512,64]{2,0,3,1:T(8,128)S(1)} fusion(f32[8,2,512,64]{2,0,3,1:T(8,128)S(1)} %fusion.39, f32[8,1,512,64]{2,0,3,1:T(8,128)S(1)} %get-tuple-element.35, f32[8,1,512,64]{2,0,3,1:T(8,128)S(1)} %get-tuple-element.34, f32[8,2,514,1]{2,0,3,1:T(8,128)S(1)} %collective-permute-done.30, f32[8,2,1,64]{2,0,3,1:T(8,128)S(1)} %collective-permute-done.28, ...), kind=kOutput, calls=%fused_computation.86 | convolution fusion | flops 66584576 | bytes 14754400 | tf_op jit(solution)/shard_map/fg,gzxy->fzxy/dot_general | solution.py:42
  296.1 1.8 reshape.20
  298.0 12.1 %reduce-scatter.10.cloned.1.call-done = f32[64,1024]{1,0:T(8,128)} async-done(((f32[128,1024]{1,0:T(8,128)}), f32[64,1024]{1,0:T(8,128)}) %reduce-scatter.10.cloned.1.call-update) | async-done | bytes 262160
  313.3 46.9 %collective-permute-done.32 = f32[8,2,512,64]{2,0,3,1:T(8,128)} collective-permute-done((f32[8,2,512,64]{2,0,3,1:T(8,128)S(1)}, f32[8,2,512,64]{2,0,3,1:T(8,128)}, u32[]{:S(2)}, u32[]{:S(2)}) %collective-permute-start.32) | collective-permute-done | bytes 2097184 | tf_op jit(solution)/shard_map/ppermute | solution.py:72
  360.2 10.5 %fusion.92 = f32[512,1024]{0,1:T(8,128)} fusion(f32[8,2,512,64]{2,0,3,1:T(8,128)S(1)} %copy-done.5, s32[]{:T(128)S(6)} %select_n.20, f32[8,2,512,64]{2,0,3,1:T(8,128)} %collective-permute-done.32), kind=kOutput, calls=%fused_computation.172 | convolution fusion | flops 6445596672 | bytes 8388612 | tf_op jit(solution)/shard_map/fzxy,fzwy->xw/dot_general | solution.py:76
  371.0 2.5 copy.69
  373.5 13.5 %all-gather.2.cloned.1.call-done = f32[8,2,64,1024]{2,0,1,3:T(8,128)} async-done(((f32[8,2,64,64]{2,0,1,3:T(8,128)}), f32[8,2,64,1024]{2,0,1,3:T(8,128)}) %all-gather.2.cloned.1.call-update) | async-done | bytes 4194320 | tf_op jit(solution)/shard_map/all_gather | solution.py:90
  387.1 6.9 %copy.66 = f32[8,2,64,1024]{3,2,1,0:T(8,128)} copy(f32[8,2,64,1024]{2,0,1,3:T(8,128)} %all-gather.2.cloned.1.call-done) | data formatting | bytes 8388608 | tf_op jit(solution)/shard_map/all_gather | solution.py:90
  394.0 5.8 %convolution_bitcast_fusion.1 = f32[64,1024]{1,0:T(8,128)} fusion(f32[8,2,64,1024]{3,2,1,0:T(8,128)} %copy.66, f32[8,2,64,64]{3,1,0,2:T(2,128)S(1)} %bitcast.93), kind=kOutput, calls=%fused_computation.174 | convolution fusion | flops 805306368 | bytes 4718592 | tf_op jit(solution)/shard_map/fzry,fzrv->yv/dot_general | solution.py:91
  399.8 51.5 %reduce-scatter.6.cloned.1.call-done = f32[512,64]{0,1:T(8,128)} async-done(((f32[512,1024]{0,1:T(8,128)}), f32[512,64]{0,1:T(8,128)}) %reduce-scatter.6.cloned.1.call-update) | async-done | bytes 131088 | tf_op jit(solution)/shard_map/reduce_scatter | solution.py:83
  451.3 1.6 broadcast_multiply_fusion.1
  452.8 5.5 %fusion.98 = f32[8,2,64,8]{2,3,1,0:T(8,128)} fusion(f32[8,2,64,1024]{3,2,1,0:T(8,128)} %copy.66, bf16[1024,128]{1,0:T(8,128)(2,1)S(1)} %copy-done.6, s32[]{:T(128)S(6)} %select_n.22), kind=kOutput, calls=%fused_computation.176 | convolution fusion | flops 100663296 | bytes 4489220 | tf_op jit(solution)/shard_map/vs,fzrv->fzrs/dot_general | solution.py:92
  458.3 5.8 %reduce-scatter.8.cloned.1.call-done = f32[64,512]{1,0:T(8,128)} async-done(((f32[64,1024]{1,0:T(8,128)}), f32[64,512]{1,0:T(8,128)}) %reduce-scatter.8.cloned.1.call-update) | async-done | bytes 131088 | tf_op jit(solution)/shard_map/reduce_scatter | solution.py:93
  464.1 1.6 broadcast_multiply_fusion
  (85 shorter events, 25.5 us)
Async XLA Ops:
  7.2 287.0 %copy-start = (bf16[1024,128]{1,0:T(8,128)(2,1)S(1)}, bf16[1024,128]{1,0:T(8,128)(2,1)}, u32[]{:S(2)}) copy-start(bf16[1024,128]{1,0:T(8,128)(2,1)} %param.10) | copy-start | bytes 786436
  7.2 302.9 %reduce-scatter.10.cloned.1.call-start = ((), (), s32[]{:S(2)}) async-start(), calls=%async_computation.6 | async-start | bytes 786432
  10.3 15.8 %collective-permute-start = (f32[8,2,1,64]{2,0,3,1:T(8,128)S(1)}, f32[8,2,1,64]{2,0,3,1:T(8,128)S(1)}, u32[]{:S(2)}, u32[]{:S(2)}) collective-permute-start(f32[8,2,1,64]{2,0,3,1:T(8,128)S(1)} %get-tuple-element.61), channel_id=1, source_target_pairs={{16,0},{0,16},{17,1},{1,17},{18,2},{2,18},{19,3},{3,19},{20,4},{4,... | collective-permute-start | bytes 12296 | tf_op jit(solution)/shard_map/ppermute | solution.py:23
  13.3 23.2 %collective-permute-start.1 = (f32[8,2,1,64]{2,0,3,1:T(8,128)S(1)}, f32[8,2,1,64]{2,0,3,1:T(8,128)S(1)}, u32[]{:S(2)}, u32[]{:S(2)}) collective-permute-start(f32[8,2,1,64]{2,0,3,1:T(8,128)S(1)} %get-tuple-element.60), channel_id=1, source_target_pairs={{0,16},{16,0},{1,17},{17,1},{2,18},{18,2},{3,19},{19,3},{4,20},{20... | collective-permute-start | bytes 12296 | tf_op jit(solution)/shard_map/ppermute | solution.py:21
  13.6 26.4 %copy-start.7 = (f32[2,8]{1,0:T(2,128)S(1)}, f32[2,8]{1,0:T(2,128)}, u32[]{:S(2)}) copy-start(f32[2,8]{1,0:T(2,128)} %param.8) | copy-start | bytes 196
  13.6 26.4 %copy-start.3 = (f32[8,2,512,64]{2,3,1,0:T(8,128)S(1)}, f32[8,2,512,64]{2,3,1,0:T(8,128)}, u32[]{:S(2)}) copy-start(f32[8,2,512,64]{2,3,1,0:T(8,128)} %param.6) | copy-start | bytes 6291460
  36.6 5.1 %collective-permute-start.2 = (f32[8,2,514,1]{2,0,3,1:T(8,128)S(1)}, f32[8,2,514,1]{2,0,3,1:T(8,128)S(1)}, u32[]{:S(2)}, u32[]{:S(2)}) collective-permute-start(f32[8,2,514,1]{2,0,3,1:T(8,128)S(1)} %get-tuple-element.31), channel_id=1, source_target_pairs={{1,0},{2,1},{3,2},{4,3},{5,4},{6,5},{7,6},{8,7},{9,8},{10,9},{11,1... | collective-permute-start | bytes 98696 | tf_op jit(solution)/shard_map/ppermute | solution.py:23
  40.0 6.1 %collective-permute-start.3 = (f32[8,2,514,1]{2,0,3,1:T(8,128)S(1)}, f32[8,2,514,1]{2,0,3,1:T(8,128)S(1)}, u32[]{:S(2)}, u32[]{:S(2)}) collective-permute-start(f32[8,2,514,1]{2,0,3,1:T(8,128)S(1)} %get-tuple-element.30), channel_id=1, source_target_pairs={{0,1},{1,2},{2,3},{3,4},{4,5},{5,6},{6,7},{7,8},{8,9},{9,10},{10,1... | collective-permute-start | bytes 98696 | tf_op jit(solution)/shard_map/ppermute | solution.py:21
  40.0 6.1 %copy-start.8 = (f32[8,8]{1,0:T(8,128)S(1)}, f32[8,8]{1,0:T(8,128)}, u32[]{:S(2)}) copy-start(f32[8,8]{1,0:T(8,128)} %param.9) | copy-start | bytes 772
  40.0 6.1 %copy-start.9 = (f32[8]{0:T(128)S(1)}, f32[8]{0:T(128)}, u32[]{:S(2)}) copy-start(f32[8]{0:T(128)} %param.7) | copy-start | bytes 100
  51.6 14.6 %collective-permute-start.4 = (f32[8,2,1,64]{2,0,3,1:T(8,128)S(1)}, f32[8,2,1,64]{2,0,3,1:T(8,128)S(1)}, u32[]{:S(2)}, u32[]{:S(2)}) collective-permute-start(f32[8,2,1,64]{2,0,3,1:T(8,128)S(1)} %get-tuple-element.57), channel_id=1, source_target_pairs={{16,0},{0,16},{17,1},{1,17},{18,2},{2,18},{19,3},{3,19},{20,4},{4,... | collective-permute-start | bytes 12296 | tf_op jit(solution)/shard_map/ppermute | solution.py:23
  53.1 18.6 %collective-permute-start.5 = (f32[8,2,1,64]{2,0,3,1:T(8,128)S(1)}, f32[8,2,1,64]{2,0,3,1:T(8,128)S(1)}, u32[]{:S(2)}, u32[]{:S(2)}) collective-permute-start(f32[8,2,1,64]{2,0,3,1:T(8,128)S(1)} %get-tuple-element.56), channel_id=1, source_target_pairs={{0,16},{16,0},{1,17},{17,1},{2,18},{18,2},{3,19},{19,3},{4,20},{20... | collective-permute-start | bytes 12296 | tf_op jit(solution)/shard_map/ppermute | solution.py:21
  71.9 5.8 %collective-permute-start.6 = (f32[8,2,514,1]{2,0,3,1:T(8,128)S(1)}, f32[8,2,514,1]{2,0,3,1:T(8,128)S(1)}, u32[]{:S(2)}, u32[]{:S(2)}) collective-permute-start(f32[8,2,514,1]{2,0,3,1:T(8,128)S(1)} %get-tuple-element.29), channel_id=1, source_target_pairs={{1,0},{2,1},{3,2},{4,3},{5,4},{6,5},{7,6},{8,7},{9,8},{10,9},{11,1... | collective-permute-start | bytes 98696 | tf_op jit(solution)/shard_map/ppermute | solution.py:23
  76.0 6.3 %collective-permute-start.7 = (f32[8,2,514,1]{2,0,3,1:T(8,128)S(1)}, f32[8,2,514,1]{2,0,3,1:T(8,128)S(1)}, u32[]{:S(2)}, u32[]{:S(2)}) collective-permute-start(f32[8,2,514,1]{2,0,3,1:T(8,128)S(1)} %get-tuple-element.28), channel_id=1, source_target_pairs={{0,1},{1,2},{2,3},{3,4},{4,5},{5,6},{6,7},{7,8},{8,9},{9,10},{10,1... | collective-permute-start | bytes 98696 | tf_op jit(solution)/shard_map/ppermute | solution.py:21
  87.0 14.6 %collective-permute-start.8 = (f32[8,2,1,64]{2,0,3,1:T(8,128)S(1)}, f32[8,2,1,64]{2,0,3,1:T(8,128)S(1)}, u32[]{:S(2)}, u32[]{:S(2)}) collective-permute-start(f32[8,2,1,64]{2,0,3,1:T(8,128)S(1)} %get-tuple-element.53), channel_id=1, source_target_pairs={{16,0},{0,16},{17,1},{1,17},{18,2},{2,18},{19,3},{3,19},{20,4},{4,... | collective-permute-start | bytes 12296 | tf_op jit(solution)/shard_map/ppermute | solution.py:23
  88.6 18.6 %collective-permute-start.9 = (f32[8,2,1,64]{2,0,3,1:T(8,128)S(1)}, f32[8,2,1,64]{2,0,3,1:T(8,128)S(1)}, u32[]{:S(2)}, u32[]{:S(2)}) collective-permute-start(f32[8,2,1,64]{2,0,3,1:T(8,128)S(1)} %get-tuple-element.52), channel_id=1, source_target_pairs={{0,16},{16,0},{1,17},{17,1},{2,18},{18,2},{3,19},{19,3},{4,20},{20... | collective-permute-start | bytes 12296 | tf_op jit(solution)/shard_map/ppermute | solution.py:21
  107.4 4.3 collective-permute-start.10
  110.0 6.1 %collective-permute-start.11 = (f32[8,2,514,1]{2,0,3,1:T(8,128)S(1)}, f32[8,2,514,1]{2,0,3,1:T(8,128)S(1)}, u32[]{:S(2)}, u32[]{:S(2)}) collective-permute-start(f32[8,2,514,1]{2,0,3,1:T(8,128)S(1)} %get-tuple-element.26), channel_id=1, source_target_pairs={{0,1},{1,2},{2,3},{3,4},{4,5},{5,6},{6,7},{7,8},{8,9},{9,10},{10,1... | collective-permute-start | bytes 98696 | tf_op jit(solution)/shard_map/ppermute | solution.py:21
  121.2 14.6 %collective-permute-start.12 = (f32[8,2,1,64]{2,0,3,1:T(8,128)S(1)}, f32[8,2,1,64]{2,0,3,1:T(8,128)S(1)}, u32[]{:S(2)}, u32[]{:S(2)}) collective-permute-start(f32[8,2,1,64]{2,0,3,1:T(8,128)S(1)} %get-tuple-element.49), channel_id=1, source_target_pairs={{16,0},{0,16},{17,1},{1,17},{18,2},{2,18},{19,3},{3,19},{20,4},{4,... | collective-permute-start | bytes 12296 | tf_op jit(solution)/shard_map/ppermute | solution.py:23
  122.8 18.6 %collective-permute-start.13 = (f32[8,2,1,64]{2,0,3,1:T(8,128)S(1)}, f32[8,2,1,64]{2,0,3,1:T(8,128)S(1)}, u32[]{:S(2)}, u32[]{:S(2)}) collective-permute-start(f32[8,2,1,64]{2,0,3,1:T(8,128)S(1)} %get-tuple-element.48), channel_id=1, source_target_pairs={{0,16},{16,0},{1,17},{17,1},{2,18},{18,2},{3,19},{19,3},{4,20},{20... | collective-permute-start | bytes 12296 | tf_op jit(solution)/shard_map/ppermute | solution.py:21
  141.5 3.0 collective-permute-start.14
  142.9 6.3 %collective-permute-start.15 = (f32[8,2,514,1]{2,0,3,1:T(8,128)S(1)}, f32[8,2,514,1]{2,0,3,1:T(8,128)S(1)}, u32[]{:S(2)}, u32[]{:S(2)}) collective-permute-start(f32[8,2,514,1]{2,0,3,1:T(8,128)S(1)} %get-tuple-element.24), channel_id=1, source_target_pairs={{0,1},{1,2},{2,3},{3,4},{4,5},{5,6},{6,7},{7,8},{8,9},{9,10},{10,1... | collective-permute-start | bytes 98696 | tf_op jit(solution)/shard_map/ppermute | solution.py:21
  154.5 14.6 %collective-permute-start.16 = (f32[8,2,1,64]{2,0,3,1:T(8,128)S(1)}, f32[8,2,1,64]{2,0,3,1:T(8,128)S(1)}, u32[]{:S(2)}, u32[]{:S(2)}) collective-permute-start(f32[8,2,1,64]{2,0,3,1:T(8,128)S(1)} %get-tuple-element.45), channel_id=1, source_target_pairs={{16,0},{0,16},{17,1},{1,17},{18,2},{2,18},{19,3},{3,19},{20,4},{4,... | collective-permute-start | bytes 12296 | tf_op jit(solution)/shard_map/ppermute | solution.py:23
  156.1 18.6 %collective-permute-start.17 = (f32[8,2,1,64]{2,0,3,1:T(8,128)S(1)}, f32[8,2,1,64]{2,0,3,1:T(8,128)S(1)}, u32[]{:S(2)}, u32[]{:S(2)}) collective-permute-start(f32[8,2,1,64]{2,0,3,1:T(8,128)S(1)} %get-tuple-element.44), channel_id=1, source_target_pairs={{0,16},{16,0},{1,17},{17,1},{2,18},{18,2},{3,19},{19,3},{4,20},{20... | collective-permute-start | bytes 12296 | tf_op jit(solution)/shard_map/ppermute | solution.py:21
  174.8 2.6 collective-permute-start.18
  175.8 6.1 %collective-permute-start.19 = (f32[8,2,514,1]{2,0,3,1:T(8,128)S(1)}, f32[8,2,514,1]{2,0,3,1:T(8,128)S(1)}, u32[]{:S(2)}, u32[]{:S(2)}) collective-permute-start(f32[8,2,514,1]{2,0,3,1:T(8,128)S(1)} %get-tuple-element.22), channel_id=1, source_target_pairs={{0,1},{1,2},{2,3},{3,4},{4,5},{5,6},{6,7},{7,8},{8,9},{9,10},{10,1... | collective-permute-start | bytes 98696 | tf_op jit(solution)/shard_map/ppermute | solution.py:21
  187.5 14.6 %collective-permute-start.20 = (f32[8,2,1,64]{2,0,3,1:T(8,128)S(1)}, f32[8,2,1,64]{2,0,3,1:T(8,128)S(1)}, u32[]{:S(2)}, u32[]{:S(2)}) collective-permute-start(f32[8,2,1,64]{2,0,3,1:T(8,128)S(1)} %get-tuple-element.41), channel_id=1, source_target_pairs={{16,0},{0,16},{17,1},{1,17},{18,2},{2,18},{19,3},{3,19},{20,4},{4,... | collective-permute-start | bytes 12296 | tf_op jit(solution)/shard_map/ppermute | solution.py:23
  189.1 18.6 %collective-permute-start.21 = (f32[8,2,1,64]{2,0,3,1:T(8,128)S(1)}, f32[8,2,1,64]{2,0,3,1:T(8,128)S(1)}, u32[]{:S(2)}, u32[]{:S(2)}) collective-permute-start(f32[8,2,1,64]{2,0,3,1:T(8,128)S(1)} %get-tuple-element.40), channel_id=1, source_target_pairs={{0,16},{16,0},{1,17},{17,1},{2,18},{18,2},{3,19},{19,3},{4,20},{20... | collective-permute-start | bytes 12296 | tf_op jit(solution)/shard_map/ppermute | solution.py:21
  207.8 2.8 collective-permute-start.22
  209.0 6.1 %collective-permute-start.23 = (f32[8,2,514,1]{2,0,3,1:T(8,128)S(1)}, f32[8,2,514,1]{2,0,3,1:T(8,128)S(1)}, u32[]{:S(2)}, u32[]{:S(2)}) collective-permute-start(f32[8,2,514,1]{2,0,3,1:T(8,128)S(1)} %get-tuple-element.20), channel_id=1, source_target_pairs={{0,1},{1,2},{2,3},{3,4},{4,5},{5,6},{6,7},{7,8},{8,9},{9,10},{10,1... | collective-permute-start | bytes 98696 | tf_op jit(solution)/shard_map/ppermute | solution.py:21
  220.9 14.6 %collective-permute-start.24 = (f32[8,2,1,64]{2,0,3,1:T(8,128)S(1)}, f32[8,2,1,64]{2,0,3,1:T(8,128)S(1)}, u32[]{:S(2)}, u32[]{:S(2)}) collective-permute-start(f32[8,2,1,64]{2,0,3,1:T(8,128)S(1)} %get-tuple-element.37), channel_id=1, source_target_pairs={{16,0},{0,16},{17,1},{1,17},{18,2},{2,18},{19,3},{3,19},{20,4},{4,... | collective-permute-start | bytes 12296 | tf_op jit(solution)/shard_map/ppermute | solution.py:23
  222.5 18.6 %collective-permute-start.25 = (f32[8,2,1,64]{2,0,3,1:T(8,128)S(1)}, f32[8,2,1,64]{2,0,3,1:T(8,128)S(1)}, u32[]{:S(2)}, u32[]{:S(2)}) collective-permute-start(f32[8,2,1,64]{2,0,3,1:T(8,128)S(1)} %get-tuple-element.36), channel_id=1, source_target_pairs={{0,16},{16,0},{1,17},{17,1},{2,18},{18,2},{3,19},{19,3},{4,20},{20... | collective-permute-start | bytes 12296 | tf_op jit(solution)/shard_map/ppermute | solution.py:21
  241.2 3.6 collective-permute-start.26
  243.1 6.5 %collective-permute-start.27 = (f32[8,2,514,1]{2,0,3,1:T(8,128)S(1)}, f32[8,2,514,1]{2,0,3,1:T(8,128)S(1)}, u32[]{:S(2)}, u32[]{:S(2)}) collective-permute-start(f32[8,2,514,1]{2,0,3,1:T(8,128)S(1)} %get-tuple-element.18), channel_id=1, source_target_pairs={{0,1},{1,2},{2,3},{3,4},{4,5},{5,6},{6,7},{7,8},{8,9},{9,10},{10,1... | collective-permute-start | bytes 98696 | tf_op jit(solution)/shard_map/ppermute | solution.py:21
  255.2 1.4 copy-start.1
  257.8 14.8 %collective-permute-start.28 = (f32[8,2,1,64]{2,0,3,1:T(8,128)}, f32[8,2,1,64]{2,0,3,1:T(8,128)S(1)}, u32[]{:S(2)}, u32[]{:S(2)}) collective-permute-start(f32[8,2,1,64]{2,0,3,1:T(8,128)} %get-tuple-element.33), channel_id=1, source_target_pairs={{16,0},{0,16},{17,1},{1,17},{18,2},{2,18},{19,3},{3,19},{20,4},{4,... | collective-permute-start | bytes 12296 | tf_op jit(solution)/shard_map/ppermute | solution.py:23
  259.3 18.8 %collective-permute-start.29 = (f32[8,2,1,64]{2,0,3,1:T(8,128)}, f32[8,2,1,64]{2,0,3,1:T(8,128)S(1)}, u32[]{:S(2)}, u32[]{:S(2)}) collective-permute-start(f32[8,2,1,64]{2,0,3,1:T(8,128)} %get-tuple-element.32), channel_id=1, source_target_pairs={{0,16},{16,0},{1,17},{17,1},{2,18},{18,2},{3,19},{19,3},{4,20},{20... | collective-permute-start | bytes 12296 | tf_op jit(solution)/shard_map/ppermute | solution.py:21
  259.8 21.0 %copy-start.2 = (f32[8,2,512,64]{2,0,3,1:T(8,128)S(1)}, f32[8,2,512,64]{2,0,3,1:T(8,128)}, u32[]{:S(2)}) copy-start(f32[8,2,512,64]{2,0,3,1:T(8,128)} %copy-done.1) | copy-start | bytes 6291460
  279.0 3.4 collective-permute-start.30
  280.8 6.1 %copy-start.10 = (f32[8,2,512,64]{2,0,3,1:T(8,128)S(1)}, f32[8,2,512,64]{2,0,3,1:T(8,128)}, u32[]{:S(2)}) copy-start(f32[8,2,512,64]{2,0,3,1:T(8,128)} %get-tuple-element.73) | copy-start | bytes 6291460
  280.8 6.1 %copy-start.11 = (f32[8,2,512,64]{2,0,3,1:T(8,128)S(1)}, f32[8,2,512,64]{2,0,3,1:T(8,128)}, u32[]{:S(2)}) copy-start(f32[8,2,512,64]{2,0,3,1:T(8,128)} %get-tuple-element.75) | copy-start | bytes 6291460
  280.8 6.1 %collective-permute-start.31 = (f32[8,2,514,1]{2,0,3,1:T(8,128)S(1)}, f32[8,2,514,1]{2,0,3,1:T(8,128)S(1)}, u32[]{:S(2)}, u32[]{:S(2)}) collective-permute-start(f32[8,2,514,1]{2,0,3,1:T(8,128)S(1)} %get-tuple-element.16), channel_id=1, source_target_pairs={{0,1},{1,2},{2,3},{3,4},{4,5},{5,6},{6,7},{7,8},{8,9},{9,10},{10,1... | collective-permute-start | bytes 98696 | tf_op jit(solution)/shard_map/ppermute | solution.py:21
  292.8 1.3 copy-start.4
  296.1 16.8 %copy-start.5 = (f32[8,2,512,64]{2,0,3,1:T(8,128)S(1)}, f32[8,2,512,64]{2,0,3,1:T(8,128)}, u32[]{:S(2)}) copy-start(f32[8,2,512,64]{2,0,3,1:T(8,128)} %copy-done.4) | copy-start | bytes 6291460
  297.9 89.2 %all-gather.2.cloned.1.call-start = ((), (), s32[]{:S(2)}) async-start(), calls=%async_computation.4 | async-start | bytes 8912896 | tf_op jit(solution)/shard_map/all_gather | solution.py:90
  312.6 138.6 %reduce-scatter.6.cloned.1.call-start = ((), (), s32[]{:S(2)}) async-start(), calls=%async_computation.3 | async-start | bytes 2228224 | tf_op jit(solution)/shard_map/reduce_scatter | solution.py:83
  312.9 47.4 %collective-permute-start.32 = (f32[8,2,512,64]{2,0,3,1:T(8,128)S(1)}, f32[8,2,512,64]{2,0,3,1:T(8,128)}, u32[]{:S(2)}, u32[]{:S(2)}) collective-permute-start(f32[8,2,512,64]{2,0,3,1:T(8,128)S(1)} %copy-done.5), channel_id=1, source_target_pairs={{0,16},{16,0},{1,17},{17,1},{2,18},{18,2},{3,19},{19,3},{4,20},{20... | collective-permute-start | bytes 6291464 | tf_op jit(solution)/shard_map/ppermute | solution.py:72
  370.7 93.3 %reduce-scatter.8.cloned.1.call-start = ((), (), s32[]{:S(2)}) async-start(), calls=%async_computation.5 | async-start | bytes 393216 | tf_op jit(solution)/shard_map/reduce_scatter | solution.py:93
  394.0 58.9 %copy-start.6 = (bf16[1024,128]{1,0:T(8,128)(2,1)S(1)}, bf16[1024,128]{1,0:T(8,128)(2,1)}, u32[]{:S(2)}) copy-start(bf16[1024,128]{1,0:T(8,128)(2,1)} %param.11) | copy-start | bytes 786436
Sparse Core Ops, SparseCore 0:
  298.0 11.9 reduce-scatter.9
  312.8 74.2 all-gather.1
  390.8 60.3 reduce-scatter.5
  453.3 10.6 reduce-scatter.7
